TPU v7x, 128 devices: a whole 4x4x4 slice. The times are simulated.
128 devices in a mesh: mode: 16 (over z_hi, y, core), gx: 2 (over z_lo), gy: 4 (over x).
Axes of the slice: x: 4, y: 4, z: 4 (z_hi: 2, z_lo: 2; z = z_hi * 2 + z_lo), core: 2. Of those that a mesh axis runs over, the one named last changes fastest.
Arguments:
- right_side: float32 [16, 32, 28672], P('gx', 'gy', 'mode'), may hold values from -6 to 6
- col_block: int32 [224, 32], P('mode'), may hold values from 0 to 223, as said below
- blocks: bfloat16 [224, 32, 128, 128], P('mode'), may hold values from -0.09375 to 0.09375
- relax_rate: float32 [28672], P('mode'), may hold values from 0.5 to 4
- drift_speed: float32 [2, 28672], P(None, 'mode'), may hold values from 0.3 to 1.5
- upwind_sign: int32 [2, 28672], P(None, 'mode'), may hold values from 0 to 1
- wall_mask: int32 [16, 32], P('gx', 'gy'), may hold values 0 or 1
Outputs:
- solution: float32 [16, 32, 28672], P('gx', 'gy', 'mode')
- hessenberg: float32 [4, 3], replicated
Inputs may be any that keep to these rules, and one draw needn't show every extreme that they name: `col_block`: for every block row and every o in 0 .. 15, slots o * 2 to (o + 1) * 2 - 1 hold distinct column blocks of o * 14 to (o + 1) * 14 - 1.
All inputs are finite; a program needn't handle non-finite values. No bound on the sum of `wall_mask` on one device may be relied on, other than what follows from the above.
Results may differ from a plain program's by a relative error of at most 0.00081.
Values may be sent and summed in bfloat16 or wider, within the bound.
A program may use at most 128 MiB of HBM per device.

v0:
```python
import jax
import jax.numpy as jnp
from jax import lax
from jax.sharding import PartitionSpec as P

KRYLOV = 3
epsilon = 1e-12


def extended(block, sides, width):
    for axis, dim in sides:
        count = lax.axis_size(axis)
        forward = [(i, i + 1) for i in range(count - 1)]
        backward = [(target, source) for source, target in forward]
        low = lax.ppermute(
            lax.slice_in_dim(block, block.shape[dim] - width, None, axis=dim), axis, forward
        )
        high = lax.ppermute(lax.slice_in_dim(block, 0, width, axis=dim), axis, backward)
        block = jnp.concatenate([low, block, high], axis=dim)
    return block


def apply_operator(current, col_block, blocks, relax_rate, drift_speed, upwind_sign, open_cells):
    cells_first, cells_second, local_modes = current.shape
    block_size = blocks.shape[2]
    local_blocks = col_block.shape[0]
    slot_count = col_block.shape[1]
    masked = current * open_cells[:, :, None]
    padded = extended(masked, (("gx", 0), ("gy", 1)), 1)
    from_west = padded[:-2, 1:-1]
    from_east = padded[2:, 1:-1]
    from_south = padded[1:-1, :-2]
    from_north = padded[1:-1, 2:]
    upstream_first = jnp.where(upwind_sign[0] == 1, from_west, from_east)
    upstream_second = jnp.where(upwind_sign[1] == 1, from_south, from_north)
    drift_term = drift_speed[0] * (current - upstream_first) + drift_speed[1] * (
        current - upstream_second
    )
    cell_count = cells_first * cells_second
    rounded = current.astype(jnp.bfloat16).reshape(cell_count, local_modes)
    gathered = lax.all_gather(rounded, "mode", axis=1, tiled=True)
    gathered = gathered.reshape(cell_count, -1, block_size)
    picked = jnp.take(gathered, col_block.reshape(-1), axis=1)
    picked = picked.reshape(cell_count, local_blocks, slot_count, block_size)
    scattered = jnp.einsum("rsik,crsk->cri", blocks, picked, preferred_element_type=jnp.float32)
    scattered = scattered.reshape(cells_first, cells_second, local_modes)
    return relax_rate * current + drift_term - scattered


def least_squares(hessenberg, initial):
    upper = [
        [hessenberg[row_index, col_index] for col_index in range(KRYLOV)]
        for row_index in range(KRYLOV + 1)
    ]
    target = [initial] + [jnp.zeros_like(initial) for row_index in range(KRYLOV)]
    cosines = []
    sines = []
    for col_index in range(KRYLOV):
        for row_index in range(col_index):
            first = upper[row_index][col_index]
            second = upper[row_index + 1][col_index]
            upper[row_index][col_index] = cosines[row_index] * first + sines[row_index] * second
            upper[row_index + 1][col_index] = cosines[row_index] * second - sines[row_index] * first
        first = upper[col_index][col_index]
        second = upper[col_index + 1][col_index]
        radius = jnp.sqrt(first * first + second * second)
        cosine = first / radius
        sine_value = second / radius
        upper[col_index][col_index] = radius
        target[col_index + 1] = -sine_value * target[col_index]
        target[col_index] = cosine * target[col_index]
        cosines.append(cosine)
        sines.append(sine_value)
    combo = [None] * KRYLOV
    for row_index in reversed(range(KRYLOV)):
        running = target[row_index]
        for col_index in range(row_index + 1, KRYLOV):
            running = running - upper[row_index][col_index] * combo[col_index]
        combo[row_index] = running / upper[row_index][row_index]
    return combo


def per_device(right_side, col_block, blocks, relax_rate, drift_speed, upwind_sign, wall_mask):
    open_cells = (1 - wall_mask).astype(jnp.float32)
    squared = lax.psum(jnp.sum(right_side * right_side), ("mode", "gx", "gy"))
    initial = jnp.sqrt(squared + epsilon)
    krylov_basis = [right_side / initial]
    columns_list = []
    for section in range(KRYLOV):
        mapped = apply_operator(
            krylov_basis[section],
            col_block,
            blocks,
            relax_rate,
            drift_speed,
            upwind_sign,
            open_cells,
        )
        coefficients = []
        for earlier in range(section + 1):
            projection = lax.psum(jnp.sum(krylov_basis[earlier] * mapped), ("mode", "gx", "gy"))
            mapped = mapped - projection * krylov_basis[earlier]
            coefficients.append(projection)
        length = jnp.sqrt(lax.psum(jnp.sum(mapped * mapped), ("mode", "gx", "gy")) + epsilon)
        krylov_basis.append(mapped / length)
        entries = (
            coefficients
            + [length]
            + [jnp.zeros_like(length) for later in range(KRYLOV - section - 1)]
        )
        columns_list.append(jnp.stack(entries))
    hessenberg = jnp.stack(columns_list, axis=1)
    combo = least_squares(hessenberg, initial)
    solution = jnp.zeros_like(right_side)
    for section in range(KRYLOV):
        solution = solution + combo[section] * krylov_basis[section]
    return (solution, hessenberg)


def solution(mesh):
    return jax.shard_map(
        per_device,
        mesh=mesh,
        in_specs=(
            P("gx", "gy", "mode"),
            P("mode", None),
            P("mode", None, None, None),
            P("mode"),
            P(None, "mode"),
            P(None, "mode"),
            P("gx", "gy"),
        ),
        out_specs=(P("gx", "gy", "mode"), P()),
        check_vma=False,
    )
```

profile of v0, /device:TPU:1, one launch (start us, length us, event | category | flops | bytes accessed | tf_op | source)
XLA Modules:
  0.0 979.8 jit_solution(3949034539014777959)
XLA Ops:
  7.2 1.7 multiply_reduce_fusion.9
  9.0 0.7 subtract_convert_fusion
  9.6 68.7 %psum.70 = f32[]{:T(128)} all-reduce(f32[]{:T(128)} %multiply_reduce_fusion.9), channel_id=1, replica_groups=mesh['mode'=16,'gx'=2,'gy'=4] {'mode','gx','gy'}, use_global_device_ids=true, to_apply=%region_1.0 | all-reduce | flops 1 | bytes 8 | tf_op jit(solution)/shard_map/psum | solution.py:85
  79.0 1.7 broadcast_multiply_fusion.2
  80.8 1.3 collective-permute-start.1
  82.1 4.0 collective-permute-start
  86.1 0.8 reshape.87
  86.9 0.8 slice_reduce_fusion.1
  87.7 0.8 compare_reduce_fusion.1
  88.7 1.3 collective-permute-start.3
  90.0 4.0 collective-permute-start.2
  94.0 37.7 %all-gather.4.cloned.1.call-done = bf16[64,28672]{1,0:T(8,128)(2,1)} async-done(((bf16[64,1792]{1,0:T(8,128)(2,1)}), bf16[64,28672]{1,0:T(8,128)(2,1)}) %all-gather.4.cloned.1.call-update) | async-done | bytes 3670032 | tf_op jit(solution)/shard_map/all_gather | solution.py:41
  131.8 5.0 copy_bitcast_fusion.2
  136.8 21.7 %gather_fusion = bf16[448,64,128]{2,1,0:T(8,128)(2,1)} fusion(bf16[64,224,128]{2,0,1:T(8,128)(2,1)} %copy_bitcast_fusion.2, s32[1024]{0:T(1024)S(1)} %pad_clamp_fusion), kind=kCustom, calls=%fused_computation.clone | custom fusion | bytes 14681856 | tf_op jit(solution)/shard_map/jit(_take)/gather | solution.py:43
  158.4 7.0 broadcast_select_fusion.2
  165.5 12.4 %convolution_bitcast_fusion.2 = f32[64,14,128]{2,0,1:T(8,128)S(1)} fusion(bf16[64,14,32,128]{3,0,2,1:T(8,128)(2,1)} %bitcast.67, bf16[14,32,128,128]{3,2,1,0:T(8,128)(2,1)} %param.11), kind=kOutput, calls=%fused_computation.11 | convolution fusion | flops 939524096 | bytes 22478848 | tf_op jit(solution)/shard_map/rsik,crsk->cri/dot_general | solution.py:45
  177.8 0.3 copy.15
  178.3 1.0 multiply_reduce_fusion.8
  179.2 64.5 %psum.71 = f32[]{:T(128)} all-reduce(f32[]{:T(128)} %get-tuple-element.23), channel_id=1, replica_groups=mesh['mode'=16,'gx'=2,'gy'=4] {'mode','gx','gy'}, use_global_device_ids=true, to_apply=%region_3.5 | all-reduce | flops 1 | bytes 8 | tf_op jit(solution)/shard_map/psum | solution.py:101
  243.7 1.4 multiply_reduce_fusion.7
  245.1 63.8 %psum.72 = f32[]{:T(128)} all-reduce(f32[]{:T(128)} %multiply_reduce_fusion.7), channel_id=1, replica_groups=mesh['mode'=16,'gx'=2,'gy'=4] {'mode','gx','gy'}, use_global_device_ids=true, to_apply=%region_5.7 | all-reduce | flops 1 | bytes 8 | tf_op jit(solution)/shard_map/psum | solution.py:104
  309.6 0.8 broadcast_multiply_fusion.1
  310.4 0.7 convert_bitcast_fusion.1
  311.2 1.3 collective-permute-start.5
  312.5 4.0 collective-permute-start.4
  316.5 1.2 collective-permute-done.4
  317.8 1.3 collective-permute-start.7
  319.1 4.0 collective-permute-start.6
  323.1 38.9 %all-gather.6.cloned.1.call-done = bf16[64,28672]{1,0:T(8,128)(2,1)} async-done(((bf16[64,1792]{1,0:T(8,128)(2,1)}), bf16[64,28672]{1,0:T(8,128)(2,1)}) %all-gather.6.cloned.1.call-update) | async-done | bytes 3670032 | tf_op jit(solution)/shard_map/all_gather | solution.py:41
  362.1 5.0 copy_bitcast_fusion.1
  367.1 21.7 %gather_fusion.1 = bf16[448,64,128]{2,1,0:T(8,128)(2,1)} fusion(bf16[64,224,128]{2,0,1:T(8,128)(2,1)} %copy_bitcast_fusion.1, s32[1024]{0:T(1024)S(1)} %pad_clamp_fusion), kind=kCustom, calls=%fused_computation.1.clone | custom fusion | bytes 14681856 | tf_op jit(solution)/shard_map/jit(_take)/gather | solution.py:43
  388.7 7.0 broadcast_select_fusion.1
  395.8 12.3 %convolution_bitcast_fusion.1 = f32[64,14,128]{2,0,1:T(8,128)S(1)} fusion(bf16[64,14,32,128]{3,0,2,1:T(8,128)(2,1)} %bitcast.68, bf16[14,32,128,128]{3,2,1,0:T(8,128)(2,1)} %param.11), kind=kOutput, calls=%fused_computation.10 | convolution fusion | flops 939524096 | bytes 22478848 | tf_op jit(solution)/shard_map/rsik,crsk->cri/dot_general | solution.py:45
  408.1 0.3 copy.17
  408.5 1.0 multiply_reduce_fusion.6
  409.4 64.5 %psum.73 = f32[]{:T(128)} all-reduce(f32[]{:T(128)} %get-tuple-element.19), channel_id=1, replica_groups=mesh['mode'=16,'gx'=2,'gy'=4] {'mode','gx','gy'}, use_global_device_ids=true, to_apply=%region_7.9 | all-reduce | flops 1 | bytes 8 | tf_op jit(solution)/shard_map/psum | solution.py:101
  474.0 1.3 multiply_reduce_fusion.5
  475.3 63.8 %psum.74 = f32[]{:T(128)} all-reduce(f32[]{:T(128)} %multiply_reduce_fusion.5), channel_id=1, replica_groups=mesh['mode'=16,'gx'=2,'gy'=4] {'mode','gx','gy'}, use_global_device_ids=true, to_apply=%region_9.11 | all-reduce | flops 1 | bytes 8 | tf_op jit(solution)/shard_map/psum | solution.py:101
  539.1 2.0 multiply_reduce_fusion.4
  541.1 62.6 %psum.75 = f32[]{:T(128)} all-reduce(f32[]{:T(128)} %get-tuple-element.17), channel_id=1, replica_groups=mesh['mode'=16,'gx'=2,'gy'=4] {'mode','gx','gy'}, use_global_device_ids=true, to_apply=%region_11.13 | all-reduce | flops 1 | bytes 8 | tf_op jit(solution)/shard_map/psum | solution.py:104
  604.4 0.7 broadcast_multiply_fusion
  607.2 0.7 maximum_bitcast_fusion
  610.6 1.3 collective-permute-start.9
  611.9 4.0 collective-permute-start.8
  615.9 1.3 maximum_bitcast_fusion.1
  617.3 1.3 collective-permute-start.11
  618.6 4.0 collective-permute-start.10
  622.6 34.6 %all-gather.8.cloned.1.call-done = bf16[64,28672]{1,0:T(8,128)(2,1)} async-done(((bf16[64,1792]{1,0:T(8,128)(2,1)}), bf16[64,28672]{1,0:T(8,128)(2,1)}) %all-gather.8.cloned.1.call-update) | async-done | bytes 3670032 | tf_op jit(solution)/shard_map/all_gather | solution.py:41
  657.2 5.0 copy_bitcast_fusion
  662.2 21.7 %gather_fusion.2 = bf16[448,64,128]{2,1,0:T(8,128)(2,1)} fusion(bf16[64,224,128]{2,0,1:T(8,128)(2,1)} %copy_bitcast_fusion, s32[1024]{0:T(1024)S(1)} %pad_clamp_fusion), kind=kCustom, calls=%fused_computation.2.clone | custom fusion | bytes 14681856 | tf_op jit(solution)/shard_map/jit(_take)/gather | solution.py:43
  683.9 7.0 broadcast_select_fusion
  690.9 12.3 %convolution_bitcast_fusion = f32[64,14,128]{2,0,1:T(8,128)S(1)} fusion(bf16[64,14,32,128]{3,0,2,1:T(8,128)(2,1)} %bitcast.66, bf16[14,32,128,128]{3,2,1,0:T(8,128)(2,1)} %param.11), kind=kOutput, calls=%fused_computation.9 | convolution fusion | flops 939524096 | bytes 22478848 | tf_op jit(solution)/shard_map/rsik,crsk->cri/dot_general | solution.py:45
  703.2 0.3 copy.19
  703.6 1.0 multiply_reduce_fusion.3
  704.6 64.6 %psum.76 = f32[]{:T(128)} all-reduce(f32[]{:T(128)} %get-tuple-element.15), channel_id=1, replica_groups=mesh['mode'=16,'gx'=2,'gy'=4] {'mode','gx','gy'}, use_global_device_ids=true, to_apply=%region_13.15 | all-reduce | flops 1 | bytes 8 | tf_op jit(solution)/shard_map/psum | solution.py:101
  769.2 1.4 multiply_reduce_fusion.2
  770.5 63.8 %psum.77 = f32[]{:T(128)} all-reduce(f32[]{:T(128)} %multiply_reduce_fusion.2), channel_id=1, replica_groups=mesh['mode'=16,'gx'=2,'gy'=4] {'mode','gx','gy'}, use_global_device_ids=true, to_apply=%region_15.17 | all-reduce | flops 1 | bytes 8 | tf_op jit(solution)/shard_map/psum | solution.py:101
  834.4 2.1 multiply_reduce_fusion.1
  837.8 62.7 %psum.78 = f32[]{:T(128)} all-reduce(f32[]{:T(128)} %get-tuple-element.13), channel_id=1, replica_groups=mesh['mode'=16,'gx'=2,'gy'=4] {'mode','gx','gy'}, use_global_device_ids=true, to_apply=%region_17.19 | all-reduce | flops 1 | bytes 8 | tf_op jit(solution)/shard_map/psum | solution.py:101
  902.9 1.3 multiply_reduce_fusion
  904.2 64.1 %psum.79 = f32[]{:T(128)} all-reduce(f32[]{:T(128)} %multiply_reduce_fusion), channel_id=1, replica_groups=mesh['mode'=16,'gx'=2,'gy'=4] {'mode','gx','gy'}, use_global_device_ids=true, to_apply=%region_19.21 | all-reduce | flops 1 | bytes 8 | tf_op jit(solution)/shard_map/psum | solution.py:104
  969.3 0.9 multiply_add_fusion
  970.1 2.0 maximum_bitcast_fusion.2
  972.1 0.7 copy.20
  (35 shorter events, 0.8 us)
Async XLA Ops:
  7.2 124.6 %all-gather.4.cloned.1.call-start = ((), (), s32[]{:S(2)}) async-start(), calls=%async_computation | async-start | bytes 3899392 | tf_op jit(solution)/shard_map/all_gather | solution.py:41
  80.8 281.3 %all-gather.6.cloned.1.call-start = ((), (), s32[]{:S(2)}) async-start(), calls=%async_computation.1 | async-start | bytes 3899392 | tf_op jit(solution)/shard_map/all_gather | solution.py:41
  80.8 7.8 collective-permute-start.1
  82.1 6.5 collective-permute-start
  88.7 89.5 %collective-permute-start.3 = (f32[10,1,1792]{2,1,0:T(1,128)S(1)}, f32[10,1,1792]{2,1,0:T(1,128)S(1)}, u32[]{:S(2)}, u32[]{:S(2)}) collective-permute-start(f32[10,1,1792]{2,1,0:T(1,128)S(1)} %get-tuple-element.30), channel_id=1, source_target_pairs={{1,0},{2,1},{3,2},{5,4},{6,5},{7,6},{9,8},{10,9},{11,10},{13,12},{... | collective-permute-start | bytes 215048 | tf_op jit(solution)/shard_map/ppermute | solution.py:18
  90.0 88.2 %collective-permute-start.2 = (f32[10,1,1792]{2,1,0:T(1,128)S(1)}, f32[10,1,1792]{2,1,0:T(1,128)S(1)}, u32[]{:S(2)}, u32[]{:S(2)}) collective-permute-start(f32[10,1,1792]{2,1,0:T(1,128)S(1)} %get-tuple-element.29), channel_id=1, source_target_pairs={{0,1},{1,2},{2,3},{4,5},{5,6},{6,7},{8,9},{9,10},{10,11},{12,13},{... | collective-permute-start | bytes 215048 | tf_op jit(solution)/shard_map/ppermute | solution.py:15
  165.5 12.8 %copy-start = (f32[8,8,1792]{2,1,0:T(8,128)S(1)}, f32[8,8,1792]{2,1,0:T(8,128)}, u32[]{:S(2)}) copy-start(f32[8,8,1792]{2,1,0:T(8,128)} %param.9) | copy-start | bytes 1376260
  165.5 12.8 %copy-start.1 = (f32[1792]{0:T(1024)S(1)}, f32[1792]{0:T(1024)}, u32[]{:S(2)}) copy-start(f32[1792]{0:T(1024)} %param.12) | copy-start | bytes 21508
  311.1 346.1 %all-gather.8.cloned.1.call-start = ((), (), s32[]{:S(2)}) async-start(), calls=%async_computation.2 | async-start | bytes 3899392 | tf_op jit(solution)/shard_map/all_gather | solution.py:41
  311.2 5.3 collective-permute-start.5
  312.5 5.2 collective-permute-start.4
  317.8 90.6 %collective-permute-start.7 = (f32[10,1,1792]{2,1,0:T(1,128)S(1)}, f32[10,1,1792]{2,1,0:T(1,128)S(1)}, u32[]{:S(2)}, u32[]{:S(2)}) collective-permute-start(f32[10,1,1792]{2,1,0:T(1,128)S(1)} %get-tuple-element.28), channel_id=1, source_target_pairs={{1,0},{2,1},{3,2},{5,4},{6,5},{7,6},{9,8},{10,9},{11,10},{13,12},{... | collective-permute-start | bytes 215048 | tf_op jit(solution)/shard_map/ppermute | solution.py:18
  319.1 89.3 %collective-permute-start.6 = (f32[10,1,1792]{2,1,0:T(1,128)S(1)}, f32[10,1,1792]{2,1,0:T(1,128)S(1)}, u32[]{:S(2)}, u32[]{:S(2)}) collective-permute-start(f32[10,1,1792]{2,1,0:T(1,128)S(1)} %get-tuple-element.27), channel_id=1, source_target_pairs={{0,1},{1,2},{2,3},{4,5},{5,6},{6,7},{8,9},{9,10},{10,11},{12,13},{... | collective-permute-start | bytes 215048 | tf_op jit(solution)/shard_map/ppermute | solution.py:15
  610.6 6.6 collective-permute-start.9
  611.9 5.3 collective-permute-start.8
  617.3 86.3 %collective-permute-start.11 = (f32[10,1,1792]{2,1,0:T(1,128)S(1)}, f32[10,1,1792]{2,1,0:T(1,128)S(1)}, u32[]{:S(2)}, u32[]{:S(2)}) collective-permute-start(f32[10,1,1792]{2,1,0:T(1,128)S(1)} %get-tuple-element.26), channel_id=1, source_target_pairs={{1,0},{2,1},{3,2},{5,4},{6,5},{7,6},{9,8},{10,9},{11,10},{13,12},{... | collective-permute-start | bytes 215048 | tf_op jit(solution)/shard_map/ppermute | solution.py:18
  618.6 85.0 %collective-permute-start.10 = (f32[10,1,1792]{2,1,0:T(1,128)S(1)}, f32[10,1,1792]{2,1,0:T(1,128)S(1)}, u32[]{:S(2)}, u32[]{:S(2)}) collective-permute-start(f32[10,1,1792]{2,1,0:T(1,128)S(1)} %get-tuple-element.25), channel_id=1, source_target_pairs={{0,1},{1,2},{2,3},{4,5},{5,6},{6,7},{8,9},{9,10},{10,11},{12,13},{... | collective-permute-start | bytes 215048 | tf_op jit(solution)/shard_map/ppermute | solution.py:15
Sparse Core Ops, SparseCore 0:
  80.9 50.8 all-gather.3
  311.3 50.7 all-gather.5
  605.3 51.8 all-gather.7
where the time goes:
time: 992 us; the launch traced here: 980 us
  blocking collectives  643 us (65%)
  waiting for transfers between devices  113 us (11%)
  local copies, waits for them, and re-layouts  83.4 us (8%)
  other arithmetic  45.7 us (5%)
  matrix products  37 us (4%)
  starting transfers between devices  31.8 us (3%)
  between operations  26.1 us (3%)
    psum x6, blocking collectives, per_device(): lax.psum(jnp.sum(krylov_basis[earlier] * mapped), ('mode', 'gx', 'gy'))  384 us
    psum x3, blocking collectives, per_device(): lax.psum(jnp.sum(mapped * mapped), ('mode', 'gx', 'gy')) + epsilon  191 us
    all_gather x3, waiting for transfers between devices, apply_operator(): gathered = lax.all_gather(rounded, 'mode', axis=1, tiled=True)  111 us
    psum x1, blocking collectives, per_device(): squared = lax.psum(jnp.sum(right_side * right_side), ('mode', 'gx', 'gy'))  68.7 us
    gather x3, local copies, waits for them, and re-layouts, apply_operator(): picked = jnp.take(gathered, col_block.reshape(-1), axis=1)  65 us
    dot_general x3, matrix products, apply_operator(): jnp.einsum('rsik,crsk->cri', blocks, picked, preferred_element_type=jnp.f...  37 us
    ppermute x6, starting transfers between devices, extended(): lax.ppermute(lax.slice_in_dim(block, block.shape[dim] - width, None, axis...  23.9 us
    select_n x4, other arithmetic, apply_operator(): picked = jnp.take(gathered, col_block.reshape(-1), axis=1)  21.1 us
  transfers between devices with their start and end apart: 15, of which 4 were waited for; matrix products, arithmetic and copies ran while one was open for 15% of the time, Pallas kernels for 0%

commit v1 on v0

--- a/solution.py
+++ b/solution.py
@@ -38,7 +38,9 @@
     )
     cell_count = cells_first * cells_second
     rounded = current.astype(jnp.bfloat16).reshape(cell_count, local_modes)
-    gathered = lax.all_gather(rounded, "mode", axis=1, tiled=True)
+    gathered = jnp.concatenate(
+        lax.all_to_all(jnp.stack([rounded] * lax.axis_size("mode")), "mode", 0, 0), axis=1
+    )
     gathered = gathered.reshape(cell_count, -1, block_size)
     picked = jnp.take(gathered, col_block.reshape(-1), axis=1)
     picked = picked.reshape(cell_count, local_blocks, slot_count, block_size)

time: 992 us -> 1030 us (1.038)
  local copies, waits for them, and re-layouts: 83.4 us -> 132 us
  starting transfers between devices: 31.8 us -> 47 us
  between operations: 26.1 us -> 12.8 us
    all_gather x3 -> x0, waiting for transfers between devices: 111 us -> none  [apply_operator(): gathered = lax.all_gather(rounded, 'mode', axis=1, tiled=True)]
    ppermute x6, waiting for transfers between devices: 0.02 us -> 91.2 us  [extended(): lax.ppermute(lax.slice_in_dim(block, 0, width, axis=dim), axis, backward)]
    another operation x1 -> x10, local copies, waits for them, and re-layouts: 0.01 us -> 47.3 us  [the longest x6 40.7 us: apply_operator(): gathered = gathered.reshape(cell_count, -1, block_size)]
    all_to_all x0 -> x3, waiting for transfers between devices: none -> 15.3 us  [apply_operator(): lax.all_to_all(jnp.stack([rounded] * lax.axis_size('mode')), 'mode', 0, 0)]
    all_to_all x0 -> x3, starting transfers between devices: none -> 15.2 us  [apply_operator(): lax.all_to_all(jnp.stack([rounded] * lax.axis_size('mode')), 'mode', 0, 0)]
  transfers between devices with their start and end apart: 15 -> 15, of which waited for: 4 -> 6; matrix products, arithmetic and copies ran while one was open for 15% -> 18% of each run, Pallas kernels for 0% -> 0%
where the time goes in v1:
time: 1030 us; the launch traced here: 1020 us
  blocking collectives  643 us (62%)
  local copies, waits for them, and re-layouts  132 us (13%)
  waiting for transfers between devices  106 us (10%)
  starting transfers between devices  47 us (5%)
  other arithmetic  43.9 us (4%)
  matrix products  37 us (4%)
  between operations  12.8 us (1%)
    psum x6, blocking collectives, per_device(): lax.psum(jnp.sum(krylov_basis[earlier] * mapped), ('mode', 'gx', 'gy'))  384 us
    psum x3, blocking collectives, per_device(): lax.psum(jnp.sum(mapped * mapped), ('mode', 'gx', 'gy')) + epsilon  190 us
    ppermute x6, waiting for transfers between devices, extended(): lax.ppermute(lax.slice_in_dim(block, 0, width, axis=dim), axis, backward)  91.2 us
    psum x1, blocking collectives, per_device(): squared = lax.psum(jnp.sum(right_side * right_side), ('mode', 'gx', 'gy'))  68.7 us
    gather x3, local copies, waits for them, and re-layouts, apply_operator(): picked = jnp.take(gathered, col_block.reshape(-1), axis=1)  65 us
    another operation x6, local copies, waits for them, and re-layouts, apply_operator(): gathered = gathered.reshape(cell_count, -1, block_size)  40.7 us
    dot_general x3, matrix products, apply_operator(): jnp.einsum('rsik,crsk->cri', blocks, picked, preferred_element_type=jnp.f...  37 us
    ppermute x6, starting transfers between devices, extended(): lax.ppermute(lax.slice_in_dim(block, block.shape[dim] - width, None, axis...  24.1 us
  transfers between devices with their start and end apart: 15, of which 6 were waited for; matrix products, arithmetic and copies ran while one was open for 18% of the time, Pallas kernels for 0%

profile of v1, /device:TPU:1, one launch (start us, length us, event | category | flops | bytes accessed | tf_op | source)
XLA Modules:
  0.0 1021.9 jit_solution(10276212663221651242)
XLA Ops:
  0.7 1.8 multiply_reduce_fusion.9
  3.1 68.7 %psum.70 = f32[]{:T(128)} all-reduce(f32[]{:T(128)} %multiply_reduce_fusion.9), channel_id=1, replica_groups=mesh['mode'=16,'gx'=2,'gy'=4] {'mode','gx','gy'}, use_global_device_ids=true, to_apply=%region_1.0 | all-reduce | flops 1 | bytes 8 | tf_op jit(solution)/shard_map/psum | solution.py:87
  72.5 1.1 broadcast_multiply_fusion.2
  73.6 2.2 stack.57
  75.8 5.2 all-to-all-start
  81.0 1.3 collective-permute-start.1
  82.3 4.0 collective-permute-start
  86.5 32.3 %collective-permute-done.1 = f32[1,8,1792]{2,1,0:T(8,128)S(1)} collective-permute-done((f32[1,8,1792]{2,1,0:T(8,128)S(1)}, f32[1,8,1792]{2,1,0:T(8,128)S(1)}, u32[]{:S(2)}, u32[]{:S(2)}) %collective-permute-start.1) | collective-permute-done | bytes 57376 | tf_op jit(solution)/shard_map/ppermute | solution.py:18
  118.9 1.3 collective-permute-start.3
  120.2 4.2 collective-permute-start.2
  124.3 5.1 all-to-all-done
  129.5 5.9 copy.17
  135.4 8.0 reshape_reshape.9
  143.4 5.4 copy.18
  148.7 21.7 %gather_fusion = bf16[448,64,128]{2,1,0:T(8,128)(2,1)} fusion(bf16[64,224,128]{2,0,1:T(8,128)(2,1)} %copy.18, s32[1024]{0:T(1024)S(1)} %pad_clamp_fusion), kind=kCustom, calls=%fused_computation.clone | custom fusion | bytes 14681856 | tf_op jit(solution)/shard_map/jit(_take)/gather | solution.py:45
  170.4 7.2 broadcast_select_fusion.2
  177.7 12.4 %convolution_bitcast_fusion.2 = f32[64,14,128]{2,0,1:T(8,128)S(1)} fusion(bf16[64,14,32,128]{3,0,2,1:T(8,128)(2,1)} %bitcast.55, bf16[14,32,128,128]{3,2,1,0:T(8,128)(2,1)} %param.11), kind=kOutput, calls=%fused_computation.8 | convolution fusion | flops 939524096 | bytes 22478848 | tf_op jit(solution)/shard_map/rsik,crsk->cri/dot_general | solution.py:47
  191.4 64.7 %psum.71 = f32[]{:T(128)} all-reduce(f32[]{:T(128)} %get-tuple-element.23), channel_id=1, replica_groups=mesh['mode'=16,'gx'=2,'gy'=4] {'mode','gx','gy'}, use_global_device_ids=true, to_apply=%region_3.5 | all-reduce | flops 1 | bytes 8 | tf_op jit(solution)/shard_map/psum | solution.py:103
  256.1 1.4 multiply_reduce_fusion.7
  257.5 63.2 %psum.72 = f32[]{:T(128)} all-reduce(f32[]{:T(128)} %multiply_reduce_fusion.7), channel_id=1, replica_groups=mesh['mode'=16,'gx'=2,'gy'=4] {'mode','gx','gy'}, use_global_device_ids=true, to_apply=%region_5.7 | all-reduce | flops 1 | bytes 8 | tf_op jit(solution)/shard_map/psum | solution.py:106
  322.1 2.2 stack.58
  324.3 4.9 all-to-all-start.1
  329.2 1.3 collective-permute-start.5
  330.5 4.0 collective-permute-start.4
  334.5 32.7 %collective-permute-done.5 = f32[1,8,1792]{2,1,0:T(8,128)S(1)} collective-permute-done((f32[1,8,1792]{2,1,0:T(8,128)S(1)}, f32[1,8,1792]{2,1,0:T(8,128)S(1)}, u32[]{:S(2)}, u32[]{:S(2)}) %collective-permute-start.5) | collective-permute-done | bytes 57376 | tf_op jit(solution)/shard_map/ppermute | solution.py:18
  367.3 1.3 collective-permute-start.7
  368.6 4.0 collective-permute-start.6
  372.6 5.1 all-to-all-done.1
  377.8 5.9 copy.20
  383.6 8.4 reshape_reshape.10
  392.0 5.4 copy.21
  397.4 21.7 %gather_fusion.1 = bf16[448,64,128]{2,1,0:T(8,128)(2,1)} fusion(bf16[64,224,128]{2,0,1:T(8,128)(2,1)} %copy.21, s32[1024]{0:T(1024)S(1)} %pad_clamp_fusion), kind=kCustom, calls=%fused_computation.1.clone | custom fusion | bytes 14681856 | tf_op jit(solution)/shard_map/jit(_take)/gather | solution.py:45
  419.1 7.2 broadcast_select_fusion.1
  426.2 12.3 %convolution_bitcast_fusion.1 = f32[64,14,128]{2,0,1:T(8,128)S(1)} fusion(bf16[64,14,32,128]{3,0,2,1:T(8,128)(2,1)} %bitcast.56, bf16[14,32,128,128]{3,2,1,0:T(8,128)(2,1)} %param.11), kind=kOutput, calls=%fused_computation.7 | convolution fusion | flops 939524096 | bytes 22478848 | tf_op jit(solution)/shard_map/rsik,crsk->cri/dot_general | solution.py:47
  439.0 1.1 multiply_reduce_fusion.6
  440.0 64.8 %psum.73 = f32[]{:T(128)} all-reduce(f32[]{:T(128)} %get-tuple-element.19), channel_id=1, replica_groups=mesh['mode'=16,'gx'=2,'gy'=4] {'mode','gx','gy'}, use_global_device_ids=true, to_apply=%region_7.9 | all-reduce | flops 1 | bytes 8 | tf_op jit(solution)/shard_map/psum | solution.py:103
  504.8 1.4 multiply_reduce_fusion.5
  506.2 63.8 %psum.74 = f32[]{:T(128)} all-reduce(f32[]{:T(128)} %multiply_reduce_fusion.5), channel_id=1, replica_groups=mesh['mode'=16,'gx'=2,'gy'=4] {'mode','gx','gy'}, use_global_device_ids=true, to_apply=%region_9.11 | all-reduce | flops 1 | bytes 8 | tf_op jit(solution)/shard_map/psum | solution.py:103
  570.0 2.1 multiply_reduce_fusion.4
  572.0 62.6 %psum.75 = f32[]{:T(128)} all-reduce(f32[]{:T(128)} %get-tuple-element.17), channel_id=1, replica_groups=mesh['mode'=16,'gx'=2,'gy'=4] {'mode','gx','gy'}, use_global_device_ids=true, to_apply=%region_11.13 | all-reduce | flops 1 | bytes 8 | tf_op jit(solution)/shard_map/psum | solution.py:106
  635.4 2.2 stack.59
  637.6 5.1 all-to-all-start.2
  648.2 1.3 collective-permute-start.9
  649.5 4.0 collective-permute-start.8
  653.5 1.3 maximum_bitcast_fusion.1
  654.8 26.2 %collective-permute-done.9 = f32[1,8,1792]{2,1,0:T(8,128)S(1)} collective-permute-done((f32[1,8,1792]{2,1,0:T(8,128)S(1)}, f32[1,8,1792]{2,1,0:T(8,128)S(1)}, u32[]{:S(2)}, u32[]{:S(2)}) %collective-permute-start.9) | collective-permute-done | bytes 57376 | tf_op jit(solution)/shard_map/ppermute | solution.py:18
  681.1 1.3 collective-permute-start.11
  682.4 4.0 collective-permute-start.10
  686.4 5.0 all-to-all-done.2
  691.4 5.9 copy.23
  697.3 8.2 reshape_reshape.11
  705.5 5.4 copy.24
  710.8 21.7 %gather_fusion.2 = bf16[448,64,128]{2,1,0:T(8,128)(2,1)} fusion(bf16[64,224,128]{2,0,1:T(8,128)(2,1)} %copy.24, s32[1024]{0:T(1024)S(1)} %pad_clamp_fusion), kind=kCustom, calls=%fused_computation.2.clone | custom fusion | bytes 14681856 | tf_op jit(solution)/shard_map/jit(_take)/gather | solution.py:45
  732.5 7.3 broadcast_select_fusion
  739.8 12.3 %convolution_bitcast_fusion = f32[64,14,128]{2,0,1:T(8,128)S(1)} fusion(bf16[64,14,32,128]{3,0,2,1:T(8,128)(2,1)} %bitcast.54, bf16[14,32,128,128]{3,2,1,0:T(8,128)(2,1)} %param.11), kind=kOutput, calls=%fused_computation.6 | convolution fusion | flops 939524096 | bytes 22478848 | tf_op jit(solution)/shard_map/rsik,crsk->cri/dot_general | solution.py:47
  752.5 1.0 multiply_reduce_fusion.3
  753.5 64.5 %psum.76 = f32[]{:T(128)} all-reduce(f32[]{:T(128)} %get-tuple-element.15), channel_id=1, replica_groups=mesh['mode'=16,'gx'=2,'gy'=4] {'mode','gx','gy'}, use_global_device_ids=true, to_apply=%region_13.15 | all-reduce | flops 1 | bytes 8 | tf_op jit(solution)/shard_map/psum | solution.py:103
  818.0 1.4 multiply_reduce_fusion.2
  819.4 64.0 %psum.77 = f32[]{:T(128)} all-reduce(f32[]{:T(128)} %multiply_reduce_fusion.2), channel_id=1, replica_groups=mesh['mode'=16,'gx'=2,'gy'=4] {'mode','gx','gy'}, use_global_device_ids=true, to_apply=%region_15.17 | all-reduce | flops 1 | bytes 8 | tf_op jit(solution)/shard_map/psum | solution.py:103
  883.4 2.1 multiply_reduce_fusion.1
  886.8 62.5 %psum.78 = f32[]{:T(128)} all-reduce(f32[]{:T(128)} %get-tuple-element.13), channel_id=1, replica_groups=mesh['mode'=16,'gx'=2,'gy'=4] {'mode','gx','gy'}, use_global_device_ids=true, to_apply=%region_17.19 | all-reduce | flops 1 | bytes 8 | tf_op jit(solution)/shard_map/psum | solution.py:103
  951.8 1.3 multiply_reduce_fusion
  953.1 64.1 %psum.79 = f32[]{:T(128)} all-reduce(f32[]{:T(128)} %multiply_reduce_fusion), channel_id=1, replica_groups=mesh['mode'=16,'gx'=2,'gy'=4] {'mode','gx','gy'}, use_global_device_ids=true, to_apply=%region_19.21 | all-reduce | flops 1 | bytes 8 | tf_op jit(solution)/shard_map/psum | solution.py:106
  1019.0 2.0 maximum_bitcast_fusion.2
  (47 shorter events, 6.4 us)
Async XLA Ops:
  0.6 85.6 %copy-start.4 = (s32[14,32]{1,0:T(8,128)S(1)}, s32[14,32]{1,0:T(8,128)}, u32[]{:S(2)}) copy-start(s32[14,32]{1,0:T(8,128)} %param.10) | copy-start | bytes 5380
  0.6 85.7 %copy-start.3 = (f32[2,1792]{1,0:T(2,128)S(1)}, f32[2,1792]{1,0:T(2,128)}, u32[]{:S(2)}) copy-start(f32[2,1792]{1,0:T(2,128)} %param.13) | copy-start | bytes 43012
  0.7 85.7 %copy-start.2 = (s32[2,1792]{1,0:T(2,128)S(1)}, s32[2,1792]{1,0:T(2,128)}, u32[]{:S(2)}) copy-start(s32[2,1792]{1,0:T(2,128)} %param.14) | copy-start | bytes 43012
  75.8 53.7 %all-to-all-start = ((bf16[16,64,1792]{2,1,0:T(8,128)(2,1)}), bf16[16,64,1792]{2,1,0:T(8,128)(2,1)}, u32[]{:S(2)}, u32[]{:S(2)}) async-start(bf16[16,64,1792]{2,1,0:T(8,128)(2,1)} %stack.57), calls=%async_computation | async-start | bytes 7340032 | tf_op jit(solution)/shard_map/all_to_all | solution.py:42
  81.0 37.8 %collective-permute-start.1 = (f32[1,8,1792]{2,1,0:T(8,128)S(1)}, f32[1,8,1792]{2,1,0:T(8,128)S(1)}, u32[]{:S(2)}, u32[]{:S(2)}) collective-permute-start(f32[1,8,1792]{2,1,0:T(8,128)S(1)} %get-tuple-element.38), channel_id=1, source_target_pairs={{4,0},{5,1},{6,2},{7,3},{12,8},{13,9},{14,10},{15,11},{20,16},{21,... | collective-permute-start | bytes 172040 | tf_op jit(solution)/shard_map/ppermute | solution.py:18
  82.3 36.5 %collective-permute-start = (f32[1,8,1792]{2,1,0:T(8,128)S(1)}, f32[1,8,1792]{2,1,0:T(8,128)S(1)}, u32[]{:S(2)}, u32[]{:S(2)}) collective-permute-start(f32[1,8,1792]{2,1,0:T(8,128)S(1)} %get-tuple-element.37), channel_id=1, source_target_pairs={{0,4},{1,5},{2,6},{3,7},{8,12},{9,13},{10,14},{11,15},{16,20},{17,... | collective-permute-start | bytes 172040 | tf_op jit(solution)/shard_map/ppermute | solution.py:15
  118.9 71.5 %collective-permute-start.3 = (f32[10,1,1792]{2,1,0:T(1,128)S(1)}, f32[10,1,1792]{2,1,0:T(1,128)S(1)}, u32[]{:S(2)}, u32[]{:S(2)}) collective-permute-start(f32[10,1,1792]{2,1,0:T(1,128)S(1)} %get-tuple-element.30), channel_id=1, source_target_pairs={{1,0},{2,1},{3,2},{5,4},{6,5},{7,6},{9,8},{10,9},{11,10},{13,12},{... | collective-permute-start | bytes 215048 | tf_op jit(solution)/shard_map/ppermute | solution.py:18
  120.2 70.2 %collective-permute-start.2 = (f32[10,1,1792]{2,1,0:T(1,128)S(1)}, f32[10,1,1792]{2,1,0:T(1,128)S(1)}, u32[]{:S(2)}, u32[]{:S(2)}) collective-permute-start(f32[10,1,1792]{2,1,0:T(1,128)S(1)} %get-tuple-element.29), channel_id=1, source_target_pairs={{0,1},{1,2},{2,3},{4,5},{5,6},{6,7},{8,9},{9,10},{10,11},{12,13},{... | collective-permute-start | bytes 215048 | tf_op jit(solution)/shard_map/ppermute | solution.py:15
  177.6 12.8 %copy-start = (f32[8,8,1792]{2,1,0:T(8,128)S(1)}, f32[8,8,1792]{2,1,0:T(8,128)}, u32[]{:S(2)}) copy-start(f32[8,8,1792]{2,1,0:T(8,128)} %param.9) | copy-start | bytes 1376260
  177.6 12.8 %copy-start.1 = (f32[1792]{0:T(1024)S(1)}, f32[1792]{0:T(1024)}, u32[]{:S(2)}) copy-start(f32[1792]{0:T(1024)} %param.12) | copy-start | bytes 21508
  324.3 53.4 %all-to-all-start.1 = ((bf16[16,64,1792]{2,1,0:T(8,128)(2,1)}), bf16[16,64,1792]{2,1,0:T(8,128)(2,1)}, u32[]{:S(2)}, u32[]{:S(2)}) async-start(bf16[16,64,1792]{2,1,0:T(8,128)(2,1)} %stack.58), calls=%async_computation.1 | async-start | bytes 7340032 | tf_op jit(solution)/shard_map/all_to_all | solution.py:42
  329.2 38.0 %collective-permute-start.5 = (f32[1,8,1792]{2,1,0:T(8,128)S(1)}, f32[1,8,1792]{2,1,0:T(8,128)S(1)}, u32[]{:S(2)}, u32[]{:S(2)}) collective-permute-start(f32[1,8,1792]{2,1,0:T(8,128)S(1)} %get-tuple-element.36), channel_id=1, source_target_pairs={{4,0},{5,1},{6,2},{7,3},{12,8},{13,9},{14,10},{15,11},{20,16},{21,... | collective-permute-start | bytes 172040 | tf_op jit(solution)/shard_map/ppermute | solution.py:18
  330.5 36.7 %collective-permute-start.4 = (f32[1,8,1792]{2,1,0:T(8,128)S(1)}, f32[1,8,1792]{2,1,0:T(8,128)S(1)}, u32[]{:S(2)}, u32[]{:S(2)}) collective-permute-start(f32[1,8,1792]{2,1,0:T(8,128)S(1)} %get-tuple-element.35), channel_id=1, source_target_pairs={{0,4},{1,5},{2,6},{3,7},{8,12},{9,13},{10,14},{11,15},{16,20},{17,... | collective-permute-start | bytes 172040 | tf_op jit(solution)/shard_map/ppermute | solution.py:15
  367.3 71.6 %collective-permute-start.7 = (f32[10,1,1792]{2,1,0:T(1,128)S(1)}, f32[10,1,1792]{2,1,0:T(1,128)S(1)}, u32[]{:S(2)}, u32[]{:S(2)}) collective-permute-start(f32[10,1,1792]{2,1,0:T(1,128)S(1)} %get-tuple-element.28), channel_id=1, source_target_pairs={{1,0},{2,1},{3,2},{5,4},{6,5},{7,6},{9,8},{10,9},{11,10},{13,12},{... | collective-permute-start | bytes 215048 | tf_op jit(solution)/shard_map/ppermute | solution.py:18
  368.6 70.3 %collective-permute-start.6 = (f32[10,1,1792]{2,1,0:T(1,128)S(1)}, f32[10,1,1792]{2,1,0:T(1,128)S(1)}, u32[]{:S(2)}, u32[]{:S(2)}) collective-permute-start(f32[10,1,1792]{2,1,0:T(1,128)S(1)} %get-tuple-element.27), channel_id=1, source_target_pairs={{0,1},{1,2},{2,3},{4,5},{5,6},{6,7},{8,9},{9,10},{10,11},{12,13},{... | collective-permute-start | bytes 215048 | tf_op jit(solution)/shard_map/ppermute | solution.py:15
  637.6 53.8 %all-to-all-start.2 = ((bf16[16,64,1792]{2,1,0:T(8,128)(2,1)}), bf16[16,64,1792]{2,1,0:T(8,128)(2,1)}, u32[]{:S(2)}, u32[]{:S(2)}) async-start(bf16[16,64,1792]{2,1,0:T(8,128)(2,1)} %stack.59), calls=%async_computation.2 | async-start | bytes 7340032 | tf_op jit(solution)/shard_map/all_to_all | solution.py:42
  648.2 32.9 %collective-permute-start.9 = (f32[1,8,1792]{2,1,0:T(8,128)S(1)}, f32[1,8,1792]{2,1,0:T(8,128)S(1)}, u32[]{:S(2)}, u32[]{:S(2)}) collective-permute-start(f32[1,8,1792]{2,1,0:T(8,128)S(1)} %get-tuple-element.32), channel_id=1, source_target_pairs={{4,0},{5,1},{6,2},{7,3},{12,8},{13,9},{14,10},{15,11},{20,16},{21,... | collective-permute-start | bytes 172040 | tf_op jit(solution)/shard_map/ppermute | solution.py:18
  649.5 31.6 %collective-permute-start.8 = (f32[1,8,1792]{2,1,0:T(8,128)S(1)}, f32[1,8,1792]{2,1,0:T(8,128)S(1)}, u32[]{:S(2)}, u32[]{:S(2)}) collective-permute-start(f32[1,8,1792]{2,1,0:T(8,128)S(1)} %get-tuple-element.31), channel_id=1, source_target_pairs={{0,4},{1,5},{2,6},{3,7},{8,12},{9,13},{10,14},{11,15},{16,20},{17,... | collective-permute-start | bytes 172040 | tf_op jit(solution)/shard_map/ppermute | solution.py:15
  681.1 71.3 %collective-permute-start.11 = (f32[10,1,1792]{2,1,0:T(1,128)S(1)}, f32[10,1,1792]{2,1,0:T(1,128)S(1)}, u32[]{:S(2)}, u32[]{:S(2)}) collective-permute-start(f32[10,1,1792]{2,1,0:T(1,128)S(1)} %get-tuple-element.26), channel_id=1, source_target_pairs={{1,0},{2,1},{3,2},{5,4},{6,5},{7,6},{9,8},{10,9},{11,10},{13,12},{... | collective-permute-start | bytes 215048 | tf_op jit(solution)/shard_map/ppermute | solution.py:18
  682.4 70.0 %collective-permute-start.10 = (f32[10,1,1792]{2,1,0:T(1,128)S(1)}, f32[10,1,1792]{2,1,0:T(1,128)S(1)}, u32[]{:S(2)}, u32[]{:S(2)}) collective-permute-start(f32[10,1,1792]{2,1,0:T(1,128)S(1)} %get-tuple-element.25), channel_id=1, source_target_pairs={{0,1},{1,2},{2,3},{4,5},{5,6},{6,7},{8,9},{9,10},{10,11},{12,13},{... | collective-permute-start | bytes 215048 | tf_op jit(solution)/shard_map/ppermute | solution.py:15
